TPU v7x, 128 devices: a whole 4x4x4 slice. The times are simulated.
128 devices in a mesh: row: 16 (over x, y), col: 8 (over z, core).
Axes of the slice: x: 4, y: 4, z: 4, core: 2. Of those that a mesh axis runs over, the one named last changes fastest.
Arguments:
- orbitals: bfloat16 [131072, 512], P(('row', 'col')), may hold values from -6 to 6
- coulomb: bfloat16 [32768, 32768], P('row', 'col'), may hold values from -0.0014648438 to 0.0014648438
- interp: bfloat16 [131072, 1024], P(('row', 'col')), may hold values from -0.1875 to 0.1875
- box_counts: int32 [128], replicated, may hold values from 1 to 768, 32768 in all
- owner_map: int32 [32768], replicated, may hold values from 0 to 32767, as said below
- grid_rows: int32 [128, 1024], P(('row', 'col')), may hold values from 0 to 1023, each once within a row
- listed: int32 [128, 1024], P(('row', 'col')), may hold values from 0 to 255
Outputs:
- exchange_action: float32 [131072, 512], P(('row', 'col'))
Inputs may be any that keep to these rules, and one draw needn't show every extreme that they name: `box_counts`: the counts sum to 32768; the largest is exactly 768. `owner_map`: A permutation of the 32768 positions; a point's owner is position // 256. No box holds more than 6 points of one owner, and the box with 768 points holds exactly 6 of some owner. `grid_rows`: each row is a permutation.
All inputs are finite; a program needn't handle non-finite values.
Results may differ from a plain program's by a relative error of at most 0.012.
Values may be sent and summed in bfloat16 or wider, within the bound.
A program may use at most 128 MiB of HBM per device.

v0:
```python
import jax
import jax.numpy as jnp
from jax import lax
from jax.sharding import PartitionSpec as P

NORB = 512
LIST = 1024
OWN = 256
SLOTS = 768
BOTH = ("row", "col")
F32 = jnp.float32
BF16 = jnp.bfloat16


def exchange(chunks):
    return lax.all_to_all(chunks, BOTH, split_axis=0, concat_axis=0, tiled=True)


def pick(index, rows, count):
    one_hot = (index[:, None] == jnp.arange(count, dtype=jnp.int32)[None, :]).astype(BF16)
    return jnp.dot(one_hot, rows, preferred_element_type=F32).astype(BF16)


def add_block(shard_rows, left_rows, kernel_tile):
    pair_tile = jnp.einsum("ak,bk->ab", left_rows, shard_rows, preferred_element_type=F32).astype(
        BF16
    )
    weighted = (pair_tile.astype(F32) * kernel_tile.astype(F32)).astype(BF16)
    return jnp.dot(weighted, shard_rows, preferred_element_type=F32)


def outgoing_chunks(orbitals, box_counts, owner_map, grid_rows, listed, my_box, box_total, lanes):
    per_owner = LIST // box_total
    box_ids = jnp.arange(box_total, dtype=jnp.int32)
    first_point = jnp.sum(jnp.where(box_ids < my_box, box_counts, 0))
    my_count = jnp.sum(jnp.where(box_ids == my_box, box_counts, 0))
    slot_ids = jnp.arange(SLOTS, dtype=jnp.int32)
    is_live = slot_ids < my_count
    padded = jnp.concatenate([owner_map, jnp.zeros((SLOTS,), jnp.int32)])
    position = lax.dynamic_slice(padded, (first_point,), (SLOTS,))
    owner_ids = position // OWN
    local_ids = position - owner_ids * OWN
    matches = (
        (owner_ids[:, None] == owner_ids[None, :])
        & is_live[None, :]
        & (slot_ids[None, :] < slot_ids[:, None])
    )
    pair_rank = jnp.sum(matches.astype(jnp.int32), axis=1)
    target = jnp.where(is_live, owner_ids * lanes + pair_rank, -1)
    dest = jnp.arange(box_total * lanes, dtype=jnp.int32)
    hits = target[None, :] == dest[:, None]
    coded = (grid_rows[0, :SLOTS] + 1) * OWN + local_ids
    found = jnp.sum(jnp.where(hits, coded[None, :], 0), axis=1)
    grid = found // OWN - 1
    local = jnp.where(found > 0, found - (grid + 1) * OWN, -1)
    picked = pick(grid, orbitals, orbitals.shape[0]).reshape(box_total, lanes, NORB)
    meta = jnp.stack(
        [listed[0].reshape(box_total, per_owner), local.reshape(box_total, lanes)], axis=1
    )
    meta = jnp.pad(meta.astype(BF16), ((0, 0), (lanes - 2, 0), (0, NORB - per_owner)))
    row_ids = jnp.arange(lanes)[None, :, None]
    return jnp.where(row_ids < lanes - 2, picked, meta)


def shards(orbitals, coulomb, interp, box_counts, owner_map, grid_rows, listed):
    box_total = lax.axis_size("row") * lax.axis_size("col")
    lanes = LIST // box_total
    my_box = lax.axis_index("row") * lax.axis_size("col") + lax.axis_index("col")
    received = exchange(
        outgoing_chunks(
            orbitals, box_counts, owner_map, grid_rows, listed, my_box, box_total, lanes
        )
    )
    wanted = received[:, lanes - 2, :lanes].astype(jnp.int32).reshape(-1)
    local = received[:, lanes - 1, :lanes].astype(jnp.int32).reshape(-1)
    place = (local[None, :] == jnp.arange(OWN, dtype=jnp.int32)[:, None]).astype(BF16)
    owned_rows = jnp.dot(
        place, received.reshape(box_total * lanes, NORB), preferred_element_type=F32
    ).astype(BF16)
    left_rows = lax.all_gather(owned_rows, "col", axis=0, tiled=True)
    column_rows = lax.all_gather(owned_rows, "row", axis=0, tiled=True)
    partial_sums = add_block(column_rows, left_rows, coulomb)
    owned_result = lax.psum_scatter(partial_sums, "col", scatter_dimension=0, tiled=True).astype(
        BF16
    )
    fetched = exchange(pick(wanted, owned_result, OWN).reshape(box_total, lanes, NORB))
    return -jnp.dot(interp, fetched.reshape(LIST, NORB), preferred_element_type=F32)


def solution(mesh):
    return jax.shard_map(
        shards,
        mesh=mesh,
        in_specs=(
            P(BOTH, None),
            P("row", "col"),
            P(BOTH, None),
            P(),
            P(),
            P(BOTH, None),
            P(BOTH, None),
        ),
        out_specs=P(BOTH, None),
        check_vma=False,
    )
```

profile of v0, /device:TPU:1, one launch (start us, length us, event | category | flops | bytes accessed | tf_op | source)
XLA Modules:
  0.0 230.3 jit_solution(10312394453121893016)
XLA Ops:
  6.5 0.0 copy-start
  6.5 0.0 all-gather.3.cloned.1.call-start
  6.5 0.8 multiply_reduce_fusion
  7.4 1.4 fusion.33
  10.2 0.7 iota_compare_fusion.14
  11.5 0.9 subtract_add_fusion
  12.4 0.4 convert_reduce_fusion
  12.8 0.7 add_select_fusion.3
  13.4 0.4 select_reduce_fusion
  13.8 0.1 reduce_sum.42
  14.0 0.1 fusion.24
  14.0 0.7 convert_reduce_fusion.1
  14.7 0.1 stack_reshape_squeeze.4
  14.8 2.5 %fusion.12 = bf16[128,8,512]{2,1,0:T(8,128)(2,1)S(1)} fusion(bf16[1024,512]{1,0:T(8,128)(2,1)} %param.7, s32[1024]{0:T(1024)S(1)} %fusion.30), kind=kOutput, calls=%fused_computation.22 | convolution fusion | flops 1075314688 | bytes 2101248 | tf_op jit(solution)/shard_map/dot_general | solution.py:21
  17.4 0.4 fusion.14
  17.8 0.6 copy.20
  18.4 30.6 %all_to_all.10 = bf16[128,8,512]{2,1,0:T(8,128)(2,1)S(1)} all-to-all(bf16[128,8,512]{2,1,0:T(8,128)(2,1)S(1)} %copy.20), channel_id=1, replica_groups=mesh['row'=16,'col'=8] {'row','col'}, dimensions={0} | all-to-all | bytes 2097152 | tf_op jit(solution)/shard_map/all_to_all | solution.py:16
  49.0 0.5 fusion.25
  49.4 0.1 reshape.161
  49.5 1.2 convolution_convert_fusion.1
  50.7 0.0 all-gather.3.cloned.1.call-update
  50.7 0.0 all-gather.5.cloned.1.call-start
  50.8 0.7 all-gather.5.cloned.1.call-update
  51.5 0.0 reduce-scatter.2.cloned.1.call-start
  51.5 21.4 %all-gather.3.cloned.1.call-done = bf16[2048,512]{1,0:T(8,128)(2,1)} async-done(((bf16[256,512]{1,0:T(8,128)(2,1)}), bf16[2048,512]{1,0:T(8,128)(2,1)}) %all-gather.3.cloned.1.call-update) | async-done | bytes 2097168 | tf_op jit(solution)/shard_map/all_gather | solution.py:80
  72.9 53.5 %all-gather.5.cloned.1.call-done = bf16[4096,512]{1,0:T(8,128)(2,1)} async-done(((bf16[256,512]{1,0:T(8,128)(2,1)}), bf16[4096,512]{1,0:T(8,128)(2,1)}) %all-gather.5.cloned.1.call-update) | async-done | bytes 4194320 | tf_op jit(solution)/shard_map/all_gather | solution.py:81
  126.4 26.1 %fusion = f32[2048,512]{1,0:T(8,128)} fusion(bf16[4096,512]{1,0:T(8,128)(2,1)} %all-gather.5.cloned.1.call-done, bf16[2048,4096]{1,0:T(8,128)(2,1)} %param.8, bf16[2048,512]{1,0:T(8,128)(2,1)} %all-gather.3.cloned.1.call-done), kind=kOutput, calls=%fused_computation.1 | convolution fusion | flops 17213423616 | bytes 27262976 | tf_op jit(solution)/shard_map/dot_general | solution.py:29
  152.5 0.0 reduce-scatter.2.cloned.1.call-update
  152.5 0.1 reshape.160
  152.6 34.9 %reduce-scatter.2.cloned.1.call-done = f32[256,512]{1,0:T(8,128)} async-done(((f32[2048,512]{1,0:T(8,128)}), f32[256,512]{1,0:T(8,128)}) %reduce-scatter.2.cloned.1.call-update) | async-done | bytes 524304 | tf_op jit(solution)/shard_map/reduce_scatter | solution.py:83
  187.5 1.5 fusion.11
  189.1 29.2 %all_to_all.11 = bf16[128,8,512]{2,1,0:T(8,128)(2,1)S(1)} all-to-all(bf16[128,8,512]{2,1,0:T(8,128)(2,1)S(1)} %fusion.11), channel_id=1, replica_groups=mesh['row'=16,'col'=8] {'row','col'}, dimensions={0} | all-to-all | bytes 2097152 | tf_op jit(solution)/shard_map/all_to_all | solution.py:16
  218.2 0.0 copy-done
  218.2 2.6 %negate_bitcast_fusion = f32[1024,512]{0,1:T(8,128)} fusion(bf16[1024,1024]{1,0:T(8,128)(2,1)S(1)} %copy-done, bf16[128,8,512]{2,1,0:T(8,128)(2,1)S(1)} %all_to_all.11), kind=kOutput, calls=%fused_computation.15 | convolution fusion | flops 1074266112 | bytes 5242880 | tf_op jit(solution)/shard_map/dot_general | solution.py:87
  220.9 2.9 %copy.21 = f32[1024,512]{1,0:T(8,128)} copy(f32[1024,512]{0,1:T(8,128)} %negate_bitcast_fusion) | data formatting | bytes 4194304 | tf_op jit(solution)/shard_map/neg | solution.py:87
  (2 shorter events, 0.0 us)
Async XLA Ops:
  6.5 211.7 %copy-start = (bf16[1024,1024]{1,0:T(8,128)(2,1)S(1)}, bf16[1024,1024]{1,0:T(8,128)(2,1)}, u32[]{:S(2)}) copy-start(bf16[1024,1024]{1,0:T(8,128)(2,1)} %param.9) | copy-start | bytes 6291460
  6.5 66.3 %all-gather.3.cloned.1.call-start = ((), (), s32[]{:S(2)}) async-start(), calls=%async_computation.3 | async-start | bytes 2359296 | tf_op jit(solution)/shard_map/all_gather | solution.py:80
  50.7 75.7 %all-gather.5.cloned.1.call-start = ((), (), s32[]{:S(2)}) async-start(), calls=%async_computation.4 | async-start | bytes 4456448 | tf_op jit(solution)/shard_map/all_gather | solution.py:81
  51.5 136.1 %reduce-scatter.2.cloned.1.call-start = ((), (), s32[]{:S(2)}) async-start(), calls=%async_computation.5 | async-start | bytes 4718592 | tf_op jit(solution)/shard_map/reduce_scatter | solution.py:83
Sparse Core Ops, SparseCore 0:
  50.8 21.9 all-gather.2
  75.0 51.3 all-gather.4
  152.7 34.8 reduce-scatter.1
where the time goes:
time: 231 us; the launch traced here: 230 us
  waiting for transfers between devices  111 us (48%)
  blocking collectives  59.8 us (26%)
  matrix products  34 us (15%)
  between operations  15.3 us (7%)
  other arithmetic  6.9 us (3%)
  local copies, waits for them, and re-layouts  3.82 us (2%)
    all_to_all x2, blocking collectives, exchange(): return lax.all_to_all(chunks, BOTH, split_axis=0, concat_axis=0, tiled=True)  59.8 us
    all_gather x1, waiting for transfers between devices, shards(): column_rows = lax.all_gather(owned_rows, 'row', axis=0, tiled=True)  53.5 us
    reduce_scatter x1, waiting for transfers between devices, shards(): lax.psum_scatter(partial_sums, 'col', scatter_dimension=0, tiled=True)  34.9 us
    dot_general x1, matrix products, add_block(): return jnp.dot(weighted, shard_rows, preferred_element_type=F32)  26.1 us
    all_gather x1, waiting for transfers between devices, shards(): left_rows = lax.all_gather(owned_rows, 'col', axis=0, tiled=True)  21.4 us
  transfers between devices with their start and end apart: 3, of which 3 were waited for; matrix products, arithmetic and copies ran while one was open for 0% of the time, Pallas kernels for 0%

commit v1 on v0

--- a/solution.py
+++ b/solution.py
@@ -77,7 +77,12 @@
     owned_rows = jnp.dot(
         place, received.reshape(box_total * lanes, NORB), preferred_element_type=F32
     ).astype(BF16)
-    left_rows = lax.all_gather(owned_rows, "col", axis=0, tiled=True)
+    ring = [owned_rows]
+    for hop in range(7):
+        ring.append(lax.ppermute(ring[-1], "col", [(dev, (dev + 1) % 8) for dev in range(8)]))
+    left_rows = jnp.roll(
+        jnp.concatenate(ring[::-1], axis=0), (lax.axis_index("col") + 1) * ring[0].shape[0], axis=0
+    )
     column_rows = lax.all_gather(owned_rows, "row", axis=0, tiled=True)
     partial_sums = add_block(column_rows, left_rows, coulomb)
     owned_result = lax.psum_scatter(partial_sums, "col", scatter_dimension=0, tiled=True).astype(

time: 231 us -> 219 us (0.948)
  waiting for transfers between devices: 111 us -> 70.9 us
  local copies, waits for them, and re-layouts: 3.82 us -> 21.8 us
  starting transfers between devices: 0.08 us -> 9.06 us
    all_gather x1, waiting for transfers between devices: 53.5 us -> 0.01 us  [shards(): column_rows = lax.all_gather(owned_rows, 'row', axis=0, tiled=True)]
    ppermute x0 -> x7, waiting for transfers between devices: none -> 35.9 us  [shards(): lax.ppermute(ring[-1], 'col', [(dev, (dev + 1) % 8) for dev in range(8)])]
    all_gather x1 -> x0, waiting for transfers between devices: 21.4 us -> none  [shards(): left_rows = lax.all_gather(owned_rows, 'col', axis=0, tiled=True)]
    unnamed x2 -> x23, local copies, waits for them, and re-layouts: 0.01 us -> 17.3 us
    ppermute x0 -> x7, starting transfers between devices: none -> 9.01 us  [shards(): lax.ppermute(ring[-1], 'col', [(dev, (dev + 1) % 8) for dev in range(8)])]
  transfers between devices with their start and end apart: 3 -> 9, of which waited for: 3 -> 8; matrix products, arithmetic and copies ran while one was open for 0% -> 8% of each run, Pallas kernels for 0% -> 0%
where the time goes in v1:
time: 219 us; the launch traced here: 218 us
  waiting for transfers between devices  70.9 us (32%)
  blocking collectives  59.7 us (27%)
  matrix products  34 us (16%)
  local copies, waits for them, and re-layouts  21.8 us (10%)
  between operations  15.6 us (7%)
  starting transfers between devices  9.06 us (4%)
  other arithmetic  6.9 us (3%)
    all_to_all x2, blocking collectives, exchange(): return lax.all_to_all(chunks, BOTH, split_axis=0, concat_axis=0, tiled=True)  59.7 us
    ppermute x7, waiting for transfers between devices, shards(): lax.ppermute(ring[-1], 'col', [(dev, (dev + 1) % 8) for dev in range(8)])  35.9 us
    reduce_scatter x1, waiting for transfers between devices, shards(): lax.psum_scatter(partial_sums, 'col', scatter_dimension=0, tiled=True)  35 us
    dot_general x1, matrix products, add_block(): return jnp.dot(weighted, shard_rows, preferred_element_type=F32)  26.1 us
    unnamed x23, local copies, waits for them, and re-layouts  17.3 us
    ppermute x7, starting transfers between devices, shards(): lax.ppermute(ring[-1], 'col', [(dev, (dev + 1) % 8) for dev in range(8)])  9.01 us
  transfers between devices with their start and end apart: 9, of which 8 were waited for; matrix products, arithmetic and copies ran while one was open for 8% of the time, Pallas kernels for 0%

profile of v1, /device:TPU:1, one launch (start us, length us, event | category | flops | bytes accessed | tf_op | source)
XLA Modules:
  0.0 217.9 jit_solution(9586580941039476610)
XLA Ops:
  6.5 1.5 fusion.35
  9.5 0.7 multiply_reduce_fusion
  10.2 0.7 iota_compare_fusion.14
  11.5 0.9 subtract_add_fusion
  12.4 0.4 convert_reduce_fusion
  12.8 0.7 add_select_fusion.3
  14.0 0.7 convert_reduce_fusion.1
  14.8 2.5 %fusion.14 = bf16[128,8,512]{2,1,0:T(8,128)(2,1)S(1)} fusion(bf16[1024,512]{1,0:T(8,128)(2,1)} %param.7, s32[1024]{0:T(1024)S(1)} %fusion.32), kind=kOutput, calls=%fused_computation.24 | convolution fusion | flops 1075314688 | bytes 2101248 | tf_op jit(solution)/shard_map/dot_general | solution.py:21
  17.4 0.4 fusion.16
  17.8 0.6 copy.20
  18.4 30.6 %all_to_all.10 = bf16[128,8,512]{2,1,0:T(8,128)(2,1)S(1)} all-to-all(bf16[128,8,512]{2,1,0:T(8,128)(2,1)S(1)} %copy.20), channel_id=1, replica_groups=mesh['row'=16,'col'=8] {'row','col'}, dimensions={0} | all-to-all | bytes 2097152 | tf_op jit(solution)/shard_map/all_to_all | solution.py:16
  49.0 0.5 fusion.27
  49.5 1.2 convolution_convert_fusion.1
  50.8 1.0 collective-permute-start
  51.8 3.6 %collective-permute-done = bf16[256,512]{1,0:T(8,128)(2,1)S(1)} collective-permute-done((bf16[256,512]{1,0:T(8,128)(2,1)}, bf16[256,512]{1,0:T(8,128)(2,1)S(1)}, u32[]{:S(2)}, u32[]{:S(2)}) %collective-permute-start) | collective-permute-done | bytes 262176 | tf_op jit(solution)/shard_map/ppermute | solution.py:82
  55.4 2.4 %collective-permute-start.1 = (bf16[256,512]{1,0:T(8,128)(2,1)S(1)}, bf16[256,512]{1,0:T(8,128)(2,1)S(1)}, u32[]{:S(2)}, u32[]{:S(2)}) collective-permute-start(bf16[256,512]{1,0:T(8,128)(2,1)S(1)} %collective-permute-done), channel_id=1, source_target_pairs={{0,1},{1,2},{2,3},{3,4},{4,5},{5,6},{6,7},{7,0},{8,9},{9,10},{10,1... | collective-permute-start | bytes 786440 | tf_op jit(solution)/shard_map/ppermute | solution.py:82
  57.8 3.3 %collective-permute-done.1 = bf16[256,512]{1,0:T(8,128)(2,1)S(1)} collective-permute-done((bf16[256,512]{1,0:T(8,128)(2,1)S(1)}, bf16[256,512]{1,0:T(8,128)(2,1)S(1)}, u32[]{:S(2)}, u32[]{:S(2)}) %collective-permute-start.1) | collective-permute-done | bytes 262176 | tf_op jit(solution)/shard_map/ppermute | solution.py:82
  61.1 2.5 %collective-permute-start.2 = (bf16[256,512]{1,0:T(8,128)(2,1)S(1)}, bf16[256,512]{1,0:T(8,128)(2,1)S(1)}, u32[]{:S(2)}, u32[]{:S(2)}) collective-permute-start(bf16[256,512]{1,0:T(8,128)(2,1)S(1)} %collective-permute-done.1), channel_id=1, source_target_pairs={{0,1},{1,2},{2,3},{3,4},{4,5},{5,6},{6,7},{7,0},{8,9},{9,10},{10,1... | collective-permute-start | bytes 786440 | tf_op jit(solution)/shard_map/ppermute | solution.py:82
  63.6 3.6 %collective-permute-done.2 = bf16[256,512]{1,0:T(8,128)(2,1)S(1)} collective-permute-done((bf16[256,512]{1,0:T(8,128)(2,1)S(1)}, bf16[256,512]{1,0:T(8,128)(2,1)S(1)}, u32[]{:S(2)}, u32[]{:S(2)}) %collective-permute-start.2) | collective-permute-done | bytes 262176 | tf_op jit(solution)/shard_map/ppermute | solution.py:82
  67.2 2.2 collective-permute-start.3
  69.4 4.8 %collective-permute-done.3 = bf16[256,512]{1,0:T(8,128)(2,1)S(1)} collective-permute-done((bf16[256,512]{1,0:T(8,128)(2,1)S(1)}, bf16[256,512]{1,0:T(8,128)(2,1)S(1)}, u32[]{:S(2)}, u32[]{:S(2)}) %collective-permute-start.3) | collective-permute-done | bytes 262176 | tf_op jit(solution)/shard_map/ppermute | solution.py:82
  74.2 1.0 collective-permute-start.4
  75.2 6.0 %collective-permute-done.4 = bf16[256,512]{1,0:T(8,128)(2,1)S(1)} collective-permute-done((bf16[256,512]{1,0:T(8,128)(2,1)S(1)}, bf16[256,512]{1,0:T(8,128)(2,1)S(1)}, u32[]{:S(2)}, u32[]{:S(2)}) %collective-permute-start.4) | collective-permute-done | bytes 262176 | tf_op jit(solution)/shard_map/ppermute | solution.py:82
  81.2 0.7 copy-done.2
  81.9 7.1 %collective-permute-done.5 = bf16[256,512]{1,0:T(8,128)(2,1)} collective-permute-done((bf16[256,512]{1,0:T(8,128)(2,1)S(1)}, bf16[256,512]{1,0:T(8,128)(2,1)}, u32[]{:S(2)}, u32[]{:S(2)}) %collective-permute-start.5) | collective-permute-done | bytes 262176 | tf_op jit(solution)/shard_map/ppermute | solution.py:82
  89.0 7.3 %collective-permute-done.6 = bf16[256,512]{1,0:T(8,128)(2,1)} collective-permute-done((bf16[256,512]{1,0:T(8,128)(2,1)}, bf16[256,512]{1,0:T(8,128)(2,1)}, u32[]{:S(2)}, u32[]{:S(2)}) %collective-permute-start.6) | collective-permute-done | bytes 262176 | tf_op jit(solution)/shard_map/ppermute | solution.py:82
  96.4 1.7 constant_dynamic-update-slice_fusion.15
  98.0 1.7 constant_dynamic-update-slice_fusion.14
  99.7 1.7 constant_dynamic-update-slice_fusion.13
  101.4 0.7 constant_dynamic-update-slice_fusion.12
  102.1 0.7 constant_dynamic-update-slice_fusion.11
  102.9 0.7 constant_dynamic-update-slice_fusion.10
  103.6 0.7 constant_dynamic-update-slice_fusion.9
  104.3 1.7 constant_dynamic-update-slice_fusion.8
  106.0 1.7 constant_dynamic-update-slice_fusion.7
  107.7 1.7 constant_dynamic-update-slice_fusion.6
  109.4 0.7 constant_dynamic-update-slice_fusion.5
  110.1 0.7 constant_dynamic-update-slice_fusion.4
  110.8 0.7 constant_dynamic-update-slice_fusion.3
  111.5 0.7 constant_dynamic-update-slice_fusion.2
  112.3 0.7 constant_dynamic-update-slice_fusion.1
  113.0 0.7 constant_dynamic-update-slice_fusion
  113.7 26.1 %fusion = f32[2048,512]{1,0:T(8,128)} fusion(bf16[4096,512]{1,0:T(8,128)(2,1)} %all-gather.2.cloned.1.call-done, bf16[2048,4096]{1,0:T(8,128)(2,1)} %param.8, bf16[4096,512]{1,0:T(8,128)(2,1)} %constant_dynamic-update-slice_fusion, s32[]{:T(128)S(6)} %select_n.80), kind=kOutput, calls=%fused_computation.1 | convolution fusion | flops 17213423616 | bytes 31457284 | tf_op jit(solution)/shard_map/dot_general | solution.py:29
  140.0 35.0 %reduce-scatter.2.cloned.1.call-done = f32[256,512]{1,0:T(8,128)} async-done(((f32[2048,512]{1,0:T(8,128)}), f32[256,512]{1,0:T(8,128)}) %reduce-scatter.2.cloned.1.call-update) | async-done | bytes 524304 | tf_op jit(solution)/shard_map/reduce_scatter | solution.py:88
  174.9 1.5 fusion.13
  176.5 29.1 %all_to_all.11 = bf16[128,8,512]{2,1,0:T(8,128)(2,1)S(1)} all-to-all(bf16[128,8,512]{2,1,0:T(8,128)(2,1)S(1)} %fusion.13), channel_id=1, replica_groups=mesh['row'=16,'col'=8] {'row','col'}, dimensions={0} | all-to-all | bytes 2097152 | tf_op jit(solution)/shard_map/all_to_all | solution.py:16
  205.6 2.6 %negate_bitcast_fusion = f32[1024,512]{0,1:T(8,128)} fusion(bf16[1024,1024]{1,0:T(8,128)(2,1)S(1)} %copy-done, bf16[128,8,512]{2,1,0:T(8,128)(2,1)S(1)} %all_to_all.11), kind=kOutput, calls=%fused_computation.15 | convolution fusion | flops 1074266112 | bytes 5242880 | tf_op jit(solution)/shard_map/dot_general | solution.py:92
  208.2 2.9 %copy.21 = f32[1024,512]{1,0:T(8,128)} copy(f32[1024,512]{0,1:T(8,128)} %negate_bitcast_fusion) | data formatting | bytes 4194304 | tf_op jit(solution)/shard_map/neg | solution.py:92
  (22 shorter events, 0.9 us)
Async XLA Ops:
  6.5 199.0 %copy-start = (bf16[1024,1024]{1,0:T(8,128)(2,1)S(1)}, bf16[1024,1024]{1,0:T(8,128)(2,1)}, u32[]{:S(2)}) copy-start(bf16[1024,1024]{1,0:T(8,128)(2,1)} %param.9) | copy-start | bytes 6291460
  6.5 107.2 %all-gather.2.cloned.1.call-start = ((), (), s32[]{:S(2)}) async-start(), calls=%async_computation.3 | async-start | bytes 4456448 | tf_op jit(solution)/shard_map/all_gather | solution.py:86
  50.7 62.3 %copy-start.1 = (bf16[256,512]{1,0:T(8,128)(2,1)S(1)}, bf16[256,512]{1,0:T(8,128)(2,1)}, u32[]{:S(2)}) copy-start(bf16[256,512]{1,0:T(8,128)(2,1)} %convolution_convert_fusion.1) | copy-start | bytes 786436
  50.7 124.2 %reduce-scatter.2.cloned.1.call-start = ((), (), s32[]{:S(2)}) async-start(), calls=%async_computation.4 | async-start | bytes 4718592 | tf_op jit(solution)/shard_map/reduce_scatter | solution.py:88
  50.8 4.6 %collective-permute-start = (bf16[256,512]{1,0:T(8,128)(2,1)}, bf16[256,512]{1,0:T(8,128)(2,1)S(1)}, u32[]{:S(2)}, u32[]{:S(2)}) collective-permute-start(bf16[256,512]{1,0:T(8,128)(2,1)} %convolution_convert_fusion.1), channel_id=1, source_target_pairs={{0,1},{1,2},{2,3},{3,4},{4,5},{5,6},{6,7},{7,0},{8,9},{9,10},{10,1... | collective-permute-start | bytes 786440 | tf_op jit(solution)/shard_map/ppermute | solution.py:82
  55.4 5.7 %collective-permute-start.1 = (bf16[256,512]{1,0:T(8,128)(2,1)S(1)}, bf16[256,512]{1,0:T(8,128)(2,1)S(1)}, u32[]{:S(2)}, u32[]{:S(2)}) collective-permute-start(bf16[256,512]{1,0:T(8,128)(2,1)S(1)} %collective-permute-done), channel_id=1, source_target_pairs={{0,1},{1,2},{2,3},{3,4},{4,5},{5,6},{6,7},{7,0},{8,9},{9,10},{10,1... | collective-permute-start | bytes 786440 | tf_op jit(solution)/shard_map/ppermute | solution.py:82
  61.1 6.1 %collective-permute-start.2 = (bf16[256,512]{1,0:T(8,128)(2,1)S(1)}, bf16[256,512]{1,0:T(8,128)(2,1)S(1)}, u32[]{:S(2)}, u32[]{:S(2)}) collective-permute-start(bf16[256,512]{1,0:T(8,128)(2,1)S(1)} %collective-permute-done.1), channel_id=1, source_target_pairs={{0,1},{1,2},{2,3},{3,4},{4,5},{5,6},{6,7},{7,0},{8,9},{9,10},{10,1... | collective-permute-start | bytes 786440 | tf_op jit(solution)/shard_map/ppermute | solution.py:82
  67.2 7.0 %collective-permute-start.3 = (bf16[256,512]{1,0:T(8,128)(2,1)S(1)}, bf16[256,512]{1,0:T(8,128)(2,1)S(1)}, u32[]{:S(2)}, u32[]{:S(2)}) collective-permute-start(bf16[256,512]{1,0:T(8,128)(2,1)S(1)} %collective-permute-done.2), channel_id=1, source_target_pairs={{0,1},{1,2},{2,3},{3,4},{4,5},{5,6},{6,7},{7,0},{8,9},{9,10},{10,1... | collective-permute-start | bytes 786440 | tf_op jit(solution)/shard_map/ppermute | solution.py:82
  74.2 7.0 %collective-permute-start.4 = (bf16[256,512]{1,0:T(8,128)(2,1)S(1)}, bf16[256,512]{1,0:T(8,128)(2,1)S(1)}, u32[]{:S(2)}, u32[]{:S(2)}) collective-permute-start(bf16[256,512]{1,0:T(8,128)(2,1)S(1)} %collective-permute-done.3), channel_id=1, source_target_pairs={{0,1},{1,2},{2,3},{3,4},{4,5},{5,6},{6,7},{7,0},{8,9},{9,10},{10,1... | collective-permute-start | bytes 786440 | tf_op jit(solution)/shard_map/ppermute | solution.py:82
  81.2 0.7 copy-start.2
  81.9 7.1 %collective-permute-start.5 = (bf16[256,512]{1,0:T(8,128)(2,1)S(1)}, bf16[256,512]{1,0:T(8,128)(2,1)}, u32[]{:S(2)}, u32[]{:S(2)}) collective-permute-start(bf16[256,512]{1,0:T(8,128)(2,1)S(1)} %collective-permute-done.4), channel_id=1, source_target_pairs={{0,1},{1,2},{2,3},{3,4},{4,5},{5,6},{6,7},{7,0},{8,9},{9,10},{10,1... | collective-permute-start | bytes 786440 | tf_op jit(solution)/shard_map/ppermute | solution.py:82
  89.0 7.3 %collective-permute-start.6 = (bf16[256,512]{1,0:T(8,128)(2,1)}, bf16[256,512]{1,0:T(8,128)(2,1)}, u32[]{:S(2)}, u32[]{:S(2)}) collective-permute-start(bf16[256,512]{1,0:T(8,128)(2,1)} %collective-permute-done.5), channel_id=1, source_target_pairs={{0,1},{1,2},{2,3},{3,4},{4,5},{5,6},{6,7},{7,0},{8,9},{9,10},{10,1... | collective-permute-start | bytes 786440 | tf_op jit(solution)/shard_map/ppermute | solution.py:82
  89.0 20.3 %copy-start.3 = (bf16[256,512]{1,0:T(8,128)(2,1)S(1)}, bf16[256,512]{1,0:T(8,128)(2,1)}, u32[]{:S(2)}) copy-start(bf16[256,512]{1,0:T(8,128)(2,1)} %copy-done.2) | copy-start | bytes 786436
Sparse Core Ops, SparseCore 0:
  50.8 47.5 all-gather.1
  140.0 34.8 reduce-scatter.1
